TPU v7x, 32 devices: a whole 2x2x4 slice. The times are simulated.
32 devices in a mesh: expert: 8 (over z, x), width: 4 (over y, core).
Axes of the slice: x: 2, y: 2, z: 4, core: 2. Of those that a mesh axis runs over, the one named last changes fastest.
Arguments:
- tokens: bfloat16 [1024, 4096], P('expert'), may hold values from -6 to 6
- expert_ids: int32 [1024, 8], P('expert'), may hold values from 0 to 15, all different within a row; in each aligned block of 128 rows (0 to 127, 128 to 255, ...) at most 128 rows name the same one
- combine_weights: float32 [1024, 8], P('expert'), may hold values from 0.05 to 0.3
- gate_weight: bfloat16 [16, 4096, 1536], P('expert', None, 'width'), may hold values from -0.09375 to 0.09375
- up_weight: bfloat16 [16, 4096, 1536], P('expert', None, 'width'), may hold values from -0.09375 to 0.09375
- down_weight: bfloat16 [16, 1536, 4096], P('expert', 'width'), may hold values from -0.15625 to 0.15625
Outputs:
- mixed: bfloat16 [1024, 4096], P('expert', 'width')
Inputs may be any that keep to these rules, and one draw needn't show every extreme that they name: `expert_ids`: each token names 8 different experts. Within the tokens of one index of expert (aligned blocks of 128 tokens) no expert is named by more than 128 tokens, a bound that some block reaches.
All inputs are finite; a program needn't handle non-finite values.
Results may differ from a plain program's by a relative error of at most 0.012.
Values may be sent and summed in bfloat16 or wider, within the bound.
A program may use at most 128 MiB of HBM per device.

v0:
```python
import jax
import jax.numpy as jnp
from jax import lax
from jax.sharding import PartitionSpec as P


def local(tokens, expert_ids, combine_weights, gate_weight, up_weight, down_weight):
    tok_rows = tokens.shape[0]
    top_count = expert_ids.shape[1]
    exp_local = gate_weight.shape[0]
    n_expert = lax.axis_size("expert")
    n_width = lax.axis_size("width")
    experts_all = exp_local * n_expert
    slots = 2 * tok_rows * top_count // experts_all
    width_all = tokens.shape[1]
    cols = width_all // n_width
    flat_ids = expert_ids.reshape(-1)
    onehot = (flat_ids[:, None] == jnp.arange(experts_all, dtype=jnp.int32)[None, :]).astype(
        jnp.int32
    )
    rank = jnp.sum(jnp.cumsum(onehot, axis=0) * onehot, axis=1) - 1
    slot = flat_ids * slots + rank
    token_index = jnp.arange(tok_rows * top_count, dtype=jnp.int32) // top_count
    table = jnp.full((experts_all * slots,), tok_rows, jnp.int32).at[slot].set(token_index)
    padded = jnp.concatenate([tokens, jnp.zeros((1, width_all), jnp.bfloat16)], axis=0)
    outgoing = padded[table].reshape(n_expert, exp_local, slots, width_all)
    own_cols = lax.dynamic_slice_in_dim(outgoing, lax.axis_index("width") * cols, cols, 3)
    arrived_cols = lax.all_to_all(own_cols, "expert", split_axis=0, concat_axis=0, tiled=True)
    arrived = lax.all_gather(arrived_cols, "width", axis=3, tiled=True)
    gate = jnp.einsum("skmd,kdf->skmf", arrived, gate_weight, preferred_element_type=jnp.float32)
    up_part = jnp.einsum("skmd,kdf->skmf", arrived, up_weight, preferred_element_type=jnp.float32)
    hidden = (jax.nn.silu(gate) * up_part).astype(jnp.bfloat16)
    partial_value = jnp.einsum(
        "skmf,kfd->skmd", hidden, down_weight, preferred_element_type=jnp.float32
    )
    reduced = lax.psum_scatter(
        partial_value.astype(jnp.bfloat16), "width", scatter_dimension=3, tiled=True
    ).astype(jnp.float32)
    returned = lax.all_to_all(
        reduced.astype(jnp.bfloat16), "expert", split_axis=0, concat_axis=0, tiled=True
    ).astype(reduced.dtype)
    picked = returned.reshape(experts_all * slots, cols)[slot].reshape(tok_rows, top_count, cols)
    mixed = jnp.sum(combine_weights[:, :, None] * picked, axis=1)
    return mixed.astype(jnp.bfloat16)


def solution(mesh):
    placed = (
        P("expert", None),
        P("expert", None),
        P("expert", None),
        P("expert", None, "width"),
        P("expert", None, "width"),
        P("expert", "width", None),
    )
    return jax.shard_map(
        local, mesh=mesh, in_specs=placed, out_specs=P("expert", "width"), check_vma=False
    )
```

profile of v0, /device:TPU:0, one launch (start us, length us, event | category | flops | bytes accessed | tf_op | source)
XLA Modules:
  0.0 540.2 jit_solution(17724048829518535215)
XLA Ops:
  6.5 0.0 all-gather.2.cloned.1.call-start
  6.5 0.8 copy.20
  7.3 0.1 eq.29
  7.4 0.1 eq.25
  7.5 0.7 broadcast_multiply_fusion
  8.2 4.5 reduce-window.6
  12.7 0.1 slice.12
  12.8 0.1 copy.22
  13.0 0.1 copy.23
  13.1 0.1 broadcast_add_fusion
  13.2 0.1 copy.19
  13.3 0.1 mul.40
  13.4 4.3 scatter_custom_fusion
  17.7 1.3 concatenate.3
  19.1 14.3 %gather_fusion = bf16[2048,4096]{1,0:T(8,128)(2,1)} fusion(bf16[129,4096]{1,0:T(8,128)(2,1)S(1)} %concatenate.3, s32[2048]{0:T(1024)S(1)} %fusion.15), kind=kCustom, calls=%fused_computation | custom fusion | bytes 33562624 | tf_op jit(solution)/shard_map/gather | solution.py:26
  33.4 2.6 constant_dynamic-slice_fusion
  36.0 100.3 %all_to_all.10 = bf16[8,2,128,1024]{3,2,1,0:T(8,128)(2,1)S(1)} all-to-all(bf16[8,2,128,1024]{3,2,1,0:T(8,128)(2,1)S(1)} %constant_dynamic-slice_fusion), channel_id=1, replica_groups=mesh['expert'=8,'width'=4] {'expert'}, dimensions={0} | all-to-all | bytes 8388608 | tf_op jit(solution)/shard_map/all_to_all | solution.py:28
  136.3 2.4 copy.24
  138.6 0.0 all-gather.2.cloned.1.call-update
  138.7 0.2 reduce-scatter.2.cloned.1.call-start
  138.9 104.9 %all-gather.2.cloned.1.call-done = bf16[8,2,128,4096]{3,2,0,1:T(8,128)(2,1)} async-done(((bf16[8,2,128,1024]{3,2,0,1:T(8,128)(2,1)}), bf16[8,2,128,4096]{3,2,0,1:T(8,128)(2,1)}) %all-gather.2.cloned.1.call-update) | async-done | bytes 16777232 | tf_op jit(solution)/shard_map/all_gather | solution.py:29
  243.8 0.0 copy-start.1
  243.8 14.1 %fusion.1 = f32[2,8,128,384]{3,2,1,0:T(8,128)S(1)} fusion(bf16[8,2,128,4096]{3,2,0,1:T(8,128)(2,1)} %all-gather.2.cloned.1.call-done, bf16[2,4096,384]{2,1,0:T(8,128)(2,1)} %param.10), kind=kOutput, calls=%fused_computation.5 | convolution fusion | flops 6442450944 | bytes 26214400 | tf_op jit(solution)/shard_map/skmd,kdf->skmf/dot_general | solution.py:31
  257.9 0.0 copy-done.1
  257.9 11.2 %fusion.6 = bf16[8,2,128,384]{3,2,0,1:T(8,128)(2,1)S(1)} fusion(f32[2,8,128,384]{3,2,1,0:T(8,128)S(1)} %fusion.1, bf16[8,2,128,4096]{3,2,0,1:T(8,128)(2,1)S(1)} %copy-done.1, bf16[2,4096,384]{2,1,0:T(8,128)(2,1)} %param.9), kind=kOutput, calls=%fused_computation.13 | convolution fusion | flops 6447169536 | bytes 27787264 | tf_op jit(solution)/shard_map/skmd,kdf->skmf/dot_general | solution.py:30
  269.2 15.2 %convert_bitcast_fusion = bf16[8,2,128,4096]{3,2,0,1:T(8,128)(2,1)} fusion(bf16[8,2,128,384]{3,2,0,1:T(8,128)(2,1)S(1)} %fusion.6, bf16[2,384,4096]{2,1,0:T(8,128)(2,1)} %param.11), kind=kOutput, calls=%fused_computation.3 | convolution fusion | flops 6450839552 | bytes 24641536 | tf_op jit(solution)/shard_map/skmf,kfd->skmd/dot_general | solution.py:33
  284.3 0.0 reduce-scatter.2.cloned.1.call-update
  284.3 125.0 %reduce-scatter.2.cloned.1.call-done = bf16[8,2,128,1024]{3,2,0,1:T(8,128)(2,1)} async-done(((bf16[8,2,128,4096]{3,2,0,1:T(8,128)(2,1)}), bf16[8,2,128,1024]{3,2,0,1:T(8,128)(2,1)}) %reduce-scatter.2.cloned.1.call-update) | async-done | bytes 4194320 | tf_op jit(solution)/shard_map/reduce_scatter | solution.py:36
  409.4 4.7 copy.25
  414.1 0.0 copy-start
  414.1 5.6 %all-to-all-start.1 = ((bf16[8,2,128,1024]{3,2,1,0:T(8,128)(2,1)}), bf16[8,2,128,1024]{3,2,1,0:T(8,128)(2,1)}, u32[]{:S(2)}, u32[]{:S(2)}) async-start(bf16[8,2,128,1024]{3,2,1,0:T(8,128)(2,1)} %copy.25), calls=%async_computation.2 | async-start | bytes 8388608 | tf_op jit(solution)/shard_map/all_to_all | solution.py:39
  419.8 0.0 copy-done
  419.8 0.1 copy.18
  419.9 93.0 %all-to-all-done.1 = bf16[8,2,128,1024]{3,2,1,0:T(8,128)(2,1)} async-done(((bf16[8,2,128,1024]{3,2,1,0:T(8,128)(2,1)}), bf16[8,2,128,1024]{3,2,1,0:T(8,128)(2,1)}, u32[]{:S(2)}, u32[]{:S(2)}) %all-to-all-start.1) | async-done | bytes 4194336 | tf_op jit(solution)/shard_map/all_to_all | solution.py:39
  512.9 6.5 %bitcast_convert_fusion = f32[2048,1024]{1,0:T(8,128)} fusion(bf16[8,2,128,1024]{3,2,1,0:T(8,128)(2,1)} %all-to-all-done.1), kind=kLoop, calls=%fused_computation.9 | loop fusion | flops 2097152 | bytes 12582912 | tf_op jit(solution)/shard_map/reshape | solution.py:42
  519.3 9.8 %gather_fusion.1 = f32[1024,1024]{1,0:T(8,128)} fusion(f32[2048,1024]{1,0:T(8,128)} %bitcast_convert_fusion, s32[1024]{0:T(1024)S(1)} %broadcast_clamp_fusion), kind=kCustom, calls=%fused_computation.1 | custom fusion | bytes 8392704 | tf_op jit(solution)/shard_map/gather | solution.py:42
  529.2 4.2 fusion.5
  (9 shorter events, 0.1 us)
Async XLA Ops:
  6.5 237.2 %all-gather.2.cloned.1.call-start = ((), (), s32[]{:S(2)}) async-start(), calls=%async_computation.3 | async-start | bytes 20971520 | tf_op jit(solution)/shard_map/all_gather | solution.py:29
  138.7 270.7 %reduce-scatter.2.cloned.1.call-start = ((), (), s32[]{:S(2)}) async-start(), calls=%async_computation.4 | async-start | bytes 20971520 | tf_op jit(solution)/shard_map/reduce_scatter | solution.py:36
  243.8 14.1 %copy-start.1 = (bf16[8,2,128,4096]{3,2,0,1:T(8,128)(2,1)S(1)}, bf16[8,2,128,4096]{3,2,0,1:T(8,128)(2,1)}, u32[]{:S(2)}) copy-start(bf16[8,2,128,4096]{3,2,0,1:T(8,128)(2,1)} %all-gather.2.cloned.1.call-done) | copy-start | bytes 50331652
  414.1 5.6 %copy-start = (f32[128,8]{0,1:T(8,128)S(1)}, f32[128,8]{0,1:T(8,128)}, u32[]{:S(2)}) copy-start(f32[128,8]{0,1:T(8,128)} %param.8) | copy-start | bytes 12292
  414.1 98.8 %all-to-all-start.1 = ((bf16[8,2,128,1024]{3,2,1,0:T(8,128)(2,1)}), bf16[8,2,128,1024]{3,2,1,0:T(8,128)(2,1)}, u32[]{:S(2)}, u32[]{:S(2)}) async-start(bf16[8,2,128,1024]{3,2,1,0:T(8,128)(2,1)} %copy.25), calls=%async_computation.2 | async-start | bytes 8388608 | tf_op jit(solution)/shard_map/all_to_all | solution.py:39
Sparse Core Ops, SparseCore 0:
  138.8 104.9 all-gather.1
  284.5 124.8 reduce-scatter.1
where the time goes:
time: 541 us; the launch traced here: 540 us
  waiting for transfers between devices  323 us (60%)
  blocking collectives  100 us (18%)
  local copies, waits for them, and re-layouts  41.1 us (8%)
  matrix products  40.5 us (7%)
  other arithmetic  16 us (3%)
  between operations  13.5 us (2%)
  starting transfers between devices  5.87 us (1%)
    reduce_scatter x1, waiting for transfers between devices, local(): lax.psum_scatter(partial_value.astype(jnp.bfloat16), 'width', scatter_dim...  125 us
    all_gather x1, waiting for transfers between devices, local(): arrived = lax.all_gather(arrived_cols, 'width', axis=3, tiled=True)  105 us
    all_to_all x1, blocking collectives, local(): lax.all_to_all(own_cols, 'expert', split_axis=0, concat_axis=0, tiled=True)  100 us
    all_to_all x1, waiting for transfers between devices, local(): lax.all_to_all(reduced.astype(jnp.bfloat16), 'expert', split_axis=0, conc...  93 us
    dot_general x1, matrix products, local(): jnp.einsum('skmf,kfd->skmd', hidden, down_weight, preferred_element_type=...  15.2 us
    gather x1, local copies, waits for them, and re-layouts, local(): outgoing = padded[table].reshape(n_expert, exp_local, slots, width_all)  14.3 us
    dot_general x1, matrix products, local(): jnp.einsum('skmd,kdf->skmf', arrived, up_weight, preferred_element_type=j...  14.1 us
    dot_general x1, matrix products, local(): jnp.einsum('skmd,kdf->skmf', arrived, gate_weight, preferred_element_type...  11.2 us
  transfers between devices with their start and end apart: 3, of which 3 were waited for; matrix products, arithmetic and copies ran while one was open for 0% of the time, Pallas kernels for 0%

commit v1 on v0

v1 whole, which is shorter than its diff:
```python
import jax
import jax.numpy as jnp
from jax import lax
from jax.sharding import PartitionSpec as P


def local(tokens, expert_ids, combine_weights, gate_weight, up_weight, down_weight):
    rows, width_all = tokens.shape
    exp_local, _, ff = gate_weight.shape
    n_expert = lax.axis_size("expert")
    n_width = lax.axis_size("width")
    experts_all = exp_local * n_expert
    cols = width_all // n_width
    part = rows // n_width
    named = expert_ids[:, :, None] == jnp.arange(experts_all, dtype=jnp.int32)
    dense = jnp.sum(jnp.where(named, combine_weights[:, :, None], 0.0), axis=1)
    dense = lax.all_gather(dense, "expert", axis=0, tiled=True)
    dense = lax.dynamic_slice_in_dim(dense, lax.axis_index("expert") * exp_local, exp_local, 1)
    own = lax.dynamic_slice_in_dim(tokens, lax.axis_index("width") * part, part, 0)
    every = lax.all_gather(own, ("expert", "width"), axis=0, tiled=True)
    gate = jnp.einsum("td,kdf->ktf", every, gate_weight, preferred_element_type=jnp.float32)
    up_part = jnp.einsum("td,kdf->ktf", every, up_weight, preferred_element_type=jnp.float32)
    hidden = (jax.nn.silu(gate) * up_part * dense.T[:, :, None]).astype(jnp.bfloat16)
    partial_value = jnp.einsum(
        "ktf,kfd->td", hidden, down_weight, preferred_element_type=jnp.float32
    ).astype(jnp.bfloat16)
    blocks = partial_value.reshape(n_expert, rows, n_width, cols).transpose(0, 2, 1, 3)
    blocks = blocks.reshape(n_expert * n_width * rows, cols)
    return lax.psum_scatter(blocks, ("expert", "width"), scatter_dimension=0, tiled=True)


def solution(mesh):
    placed = (
        P("expert", None),
        P("expert", None),
        P("expert", None),
        P("expert", None, "width"),
        P("expert", None, "width"),
        P("expert", "width", None),
    )
    return jax.shard_map(
        local, mesh=mesh, in_specs=placed, out_specs=P("expert", "width"), check_vma=False
    )
```

time: 541 us -> 309 us (0.57)
  waiting for transfers between devices: 323 us -> 198 us
  blocking collectives: 100 us -> 32.4 us
  other arithmetic: 16 us -> 0.74 us
  local copies, waits for them, and re-layouts: 41.1 us -> 26.3 us
  starting transfers between devices: 5.87 us -> 0.04 us
    all_to_all x1 -> x0, blocking collectives: 100 us -> none  [local(): lax.all_to_all(own_cols, 'expert', split_axis=0, concat_axis=0, tiled=True)]
    all_to_all x1 -> x0, waiting for transfers between devices: 93 us -> none  [local(): lax.all_to_all(reduced.astype(jnp.bfloat16), 'expert', split_axis=0, conc...]
    all_gather x1, waiting for transfers between devices: 105 us -> 48.4 us  [local(): every = lax.all_gather(own, ('expert', 'width'), axis=0, tiled=True)]
    all_gather x0 -> x1, blocking collectives: none -> 32.4 us  [local(): dense = lax.all_gather(dense, 'expert', axis=0, tiled=True)]
    gather x2 -> x0, local copies, waits for them, and re-layouts: 24.1 us -> none  [the longest x1 14.3 us: local(): outgoing = padded[table].reshape(n_expert, exp_local, slots, width_all)]
    reduce_scatter x1, waiting for transfers between devices: 125 us -> 149 us  [local(): lax.psum_scatter(blocks, ('expert', 'width'), scatter_dimension=0, tiled=...]
    reshape x0 -> x1, local copies, waits for them, and re-layouts: none -> 14.6 us  [local(): partial_value.reshape(n_expert, rows, n_width, cols).transpose(0, 2, 1, 3)]
    transpose x0 -> x2, local copies, waits for them, and re-layouts: none -> 9.78 us  [the longest x1 9.77 us: local(): partial_value.reshape(n_expert, rows, n_width, cols).transpose(0, 2, 1, 3)]
  transfers between devices with their start and end apart: 3 -> 2, of which waited for: 3 -> 2; matrix products, arithmetic and copies ran while one was open for 0% -> 0% of each run, Pallas kernels for 0% -> 0%
where the time goes in v1:
time: 309 us
  waiting for transfers between devices  198 us (64%)
  matrix products  38.1 us (12%)
  blocking collectives  32.4 us (10%)
  local copies, waits for them, and re-layouts  26.3 us (9%)
  between operations  13.4 us (4%)
    reduce_scatter x1, waiting for transfers between devices, local(): lax.psum_scatter(blocks, ('expert', 'width'), scatter_dimension=0, tiled=...  149 us
    all_gather x1, waiting for transfers between devices, local(): every = lax.all_gather(own, ('expert', 'width'), axis=0, tiled=True)  48.4 us
    all_gather x1, blocking collectives, local(): dense = lax.all_gather(dense, 'expert', axis=0, tiled=True)  32.4 us
    dot_general x1, matrix products, local(): jnp.einsum('ktf,kfd->td', hidden, down_weight, preferred_element_type=jnp...  26 us
    reshape x1, local copies, waits for them, and re-layouts, local(): partial_value.reshape(n_expert, rows, n_width, cols).transpose(0, 2, 1, 3)  14.6 us
    dot_general x1, matrix products, local(): jnp.einsum('td,kdf->ktf', every, up_weight, preferred_element_type=jnp.fl...  12.1 us
    transpose x1, local copies, waits for them, and re-layouts, local(): partial_value.reshape(n_expert, rows, n_width, cols).transpose(0, 2, 1, 3)  9.77 us
  transfers between devices with their start and end apart: 2, of which 2 were waited for; matrix products, arithmetic and copies ran while one was open for 0% of the time, Pallas kernels for 0%

profile of v1, /device:TPU:0, one launch (start us, length us, event | category | flops | bytes accessed | tf_op | source)
XLA Modules:
  0.0 308.6 jit_solution(11914623895623492090)
XLA Ops:
  6.5 0.0 copy-start
  6.5 0.0 all-gather.2.cloned.1.call-start
  6.5 1.2 copy-done
  7.8 0.7 constant_dynamic-slice_fusion
  8.5 0.0 all-gather.2.cloned.1.call-update
  8.5 0.0 reduce-scatter.2.cloned.1.call-start
  8.6 0.7 select_reduce_fusion
  9.3 32.4 %all_gather.7 = f32[1024,16]{0,1:T(8,128)S(1)} all-gather(f32[128,16]{0,1:T(8,128)S(1)} %select_reduce_fusion), channel_id=1, replica_groups=mesh['expert'=8,'width'=4] {'expert'}, dimensions={0}, use_global_device_ids=true | all-gather | bytes 73728 | tf_op jit(solution)/shard_map/all_gather | solution.py:17
  41.7 48.4 %all-gather.2.cloned.1.call-done = bf16[1024,4096]{1,0:T(8,128)(2,1)} async-done(((bf16[32,4096]{1,0:T(8,128)(2,1)}), bf16[1024,4096]{1,0:T(8,128)(2,1)}) %all-gather.2.cloned.1.call-update) | async-done | bytes 8388624 | tf_op jit(solution)/shard_map/all_gather | solution.py:20
  90.1 12.1 %fusion = f32[1024,2,384]{2,0,1:T(8,128)} fusion(bf16[2,4096,384]{2,1,0:T(8,128)(2,1)} %param.10, bf16[1024,4096]{1,0:T(8,128)(2,1)} %all-gather.2.cloned.1.call-done), kind=kOutput, calls=%fused_computation.1 | convolution fusion | flops 6442450944 | bytes 17825792 | tf_op jit(solution)/shard_map/td,kdf->ktf/dot_general | solution.py:22
  102.2 26.0 %bitcast_convert_fusion = bf16[1024,4096]{1,0:T(8,128)(2,1)} fusion(bf16[2,384,4096]{2,1,0:T(8,128)(2,1)} %param.11, f32[1024,2,384]{2,0,1:T(8,128)} %fusion, bf16[2,4096,384]{2,1,0:T(8,128)(2,1)} %param.9, bf16[1024,4096]{1,0:T(8,128)(2,1)} %all-gather.2.cloned.1.call-done, f32[2,1024]{1,0:T(2,128)S(1)} %dynamic-slice_bitcast_fusion), kind=kOutput, calls=%fused_computation | convolution fusion | flops 12894601216 | bytes 32514048 | tf_op jit(solution)/shard_map/ktf,kfd->td/dot_general | solution.py:24
  128.2 14.6 %reshape.9 = bf16[8,128,4,1024]{3,2,1,0:T(4,128)(2,1)} reshape(bf16[1024,4096]{1,0:T(8,128)(2,1)} %bitcast_convert_fusion) | data formatting | bytes 16777216 | tf_op jit(solution)/shard_map/reshape | solution.py:27
  142.8 9.8 %copy.10 = bf16[8,4,128,1024]{3,2,1,0:T(8,128)(2,1)} copy(bf16[8,4,128,1024]{3,1,2,0:T(4,128)(2,1)} %bitcast.42) | data formatting | bytes 16777216 | tf_op jit(solution)/shard_map/transpose | solution.py:27
  152.5 0.0 reduce-scatter.2.cloned.1.call-update
  152.6 149.2 %reduce-scatter.2.cloned.1.call-done = bf16[128,1024]{1,0:T(8,128)(2,1)} async-done(((bf16[4096,1024]{1,0:T(8,128)(2,1)}), bf16[128,1024]{1,0:T(8,128)(2,1)}) %reduce-scatter.2.cloned.1.call-update) | async-done | bytes 262160 | tf_op jit(solution)/shard_map/reduce_scatter | solution.py:29
  (1 shorter events, 0.0 us)
Async XLA Ops:
  6.5 1.2 copy-start
  6.5 83.6 %all-gather.2.cloned.1.call-start = ((), (), s32[]{:S(2)}) async-start(), calls=%async_computation.1 | async-start | bytes 8650752 | tf_op jit(solution)/shard_map/all_gather | solution.py:20
  8.5 293.2 %reduce-scatter.2.cloned.1.call-start = ((), (), s32[]{:S(2)}) async-start(), calls=%async_computation.2 | async-start | bytes 8650752 | tf_op jit(solution)/shard_map/reduce_scatter | solution.py:29
Sparse Core Ops, SparseCore 0:
  10.2 79.8 all-gather.1
  152.7 148.9 reduce-scatter.1

commit v2 on v1

v2 whole, which is shorter than its diff:
```python
import functools

import jax
import jax.numpy as jnp
from jax import lax
from jax.experimental import pallas as pl
from jax.experimental.pallas import tpu as pltpu
from jax.sharding import PartitionSpec as P

LANE = 128
F32 = jnp.float32


def kernel(nz, shared, single, exp_local, rows, width_all, ff,
           x_ref, g_hbm, u_hbm, d_hbm, out_ref, land,
           gw, uw, dw, xbuf, acc, hid, part, r1, ys, xs, yr2, xr2, x3s, y3s, x3r, y3r,
           zsb, zr4, wsem, lsem, zs, zr, xsnd, xr, ysnd, yr, csnd, cr,
           s1s, s1r, s2s, s2r, s3s, s3r, s4s, s4r):
    e, w = lax.axis_index("expert"), lax.axis_index("width")
    z, x = e // 2, e % 2
    y, c = w // 2, w % 2
    cols = width_all // 4
    half = cols // 2
    xdev = (z * 2 + 1 - x, w)
    ydev = (e, (1 - y) * 2 + c)
    cdev = (e, y * 2 + 1 - c)

    def zdev(q):
        return ((z + q) % nz) * 2 + x, w

    weights = [
        pltpu.make_async_copy(src, dst, wsem.at[i])
        for i, (src, dst) in enumerate(((g_hbm, gw), (u_hbm, uw), (d_hbm, dw)))
    ]
    for copy in weights:
        copy.start()

    barrier = pltpu.get_barrier_semaphore()
    peers = [zdev(q) for q in range(1, nz)] + [xdev, ydev, cdev]
    for peer in peers:
        pl.semaphore_signal(barrier, inc=1, device_id=peer, device_id_type=pl.DeviceIdType.MESH)
    pl.semaphore_wait(barrier, len(peers))

    def remote(src, dst, send, recv, dev):
        return pltpu.make_async_remote_copy(
            src_ref=src, dst_ref=dst, send_sem=send, recv_sem=recv,
            device_id=dev, device_id_type=pl.DeviceIdType.MESH)

    sends = []

    def go(copy):
        copy.start()
        sends.append(copy)

    def span(kind, owner):
        if kind == 0:
            return pl.ds(pl.multiple_of(owner * shared, LANE), shared)
        return pl.ds(pl.multiple_of(4 * shared + owner * single, LANE), single)

    own_span = (span(0, w), span(1, c))
    y_span = span(0, (1 - y) * 2 + c)

    def block(p, j):
        return ((z + p) % nz) * 2 + (x if j == 0 else 1 - x)

    def source(p, j, cut):
        if p == 0 and j == 0:
            return x_ref.at[:, cut]
        return land.at[block(p, j), :, cut]

    def send_own():
        for i in range(2):
            go(remote(x_ref.at[:, own_span[i]], land.at[e, :, own_span[i]],
                      xsnd.at[0, i], xr.at[0, i], xdev))
        for q in range(1, nz):
            for i in range(2):
                go(remote(x_ref.at[:, own_span[i]], land.at[e, :, own_span[i]],
                          zs.at[q, i], zr.at[nz - q, i], zdev(q)))

    def spread(p, j):
        ref = land.at[block(p, j), :, own_span[0]]
        go(remote(ref, ref, ysnd.at[p, j], yr.at[p, j], ydev))
        for i in range(2):
            ref = land.at[block(p, j), :, own_span[i]]
            go(remote(ref, ref, csnd.at[p, j, i], cr.at[p, j, i], cdev))

    def take_z(p):
        for i in range(2):
            ref = land.at[block(p, 0), :, own_span[i]]
            remote(ref, ref, zs.at[0, i], zr.at[p, i], xdev).wait_recv()
            go(remote(ref, ref, xsnd.at[p, i], xr.at[p, i], xdev))
        spread(p, 0)

    def take_x(p):
        for i in range(2):
            ref = land.at[block(p, 1), :, own_span[i]]
            remote(ref, ref, zs.at[0, i], xr.at[p, i], xdev).wait_recv()
        spread(p, 1)

    def blocks_of(p):
        return (1,) if p == 0 else (0, 1)

    def take_y(p):
        for j in blocks_of(p):
            ref = land.at[block(p, j), :, y_span]
            remote(ref, ref, zs.at[0, 0], yr.at[p, j], ydev).wait_recv()
            go(remote(ref, ref, csnd.at[p, j, 2], cr.at[p, j, 2], cdev))

    def take_c(p):
        other = (span(0, y * 2 + 1 - c), span(1, 1 - c), span(0, (1 - y) * 2 + 1 - c))
        for j in blocks_of(p):
            for i in range(3):
                ref = land.at[block(p, j), :, other[i]]
                remote(ref, ref, zs.at[0, 0], cr.at[p, j, i], cdev).wait_recv()
        for j in blocks_of(p):
            pltpu.make_async_copy(land.at[block(p, j)], xbuf.at[p % 2, j], lsem.at[j]).start()

    def load_wait(p):
        for j in blocks_of(p):
            pltpu.make_async_copy(land.at[block(p, j)], xbuf.at[p % 2, j], lsem.at[j]).wait()

    def mine(yy):
        return pl.multiple_of((2 * (y if yy == 0 else 1 - y) + c) * cols, LANE)

    stage1, stage2, stage3, stage4 = {}, {}, {}, {}

    def send1(p):
        stage1[p] = []
        for yy in range(2):
            begin = pl.multiple_of((2 * (y if yy == 0 else 1 - y) + 1 - c) * cols, LANE)
            copy = remote(part.at[p % 2, :, :, pl.ds(begin, cols)], r1.at[p, yy],
                          s1s.at[p, yy], s1r.at[p, yy], cdev)
            copy.start()
            stage1[p].append(copy)

    def sum1(p, yy, jj, begin):
        return (part[p % 2, jj, :, pl.ds(pl.multiple_of(mine(yy) + begin, LANE), half)].astype(F32)
                + r1[p, yy, jj, :, pl.ds(begin, half)].astype(F32))

    def do1(p):
        for copy in stage1[p]:
            copy.wait()
        s = p % 2
        if p >= 2:
            for copy in stage2[p - 2]:
                copy.wait_send()
        for i in range(2):
            ys[s, i] = sum1(p, 1, i, 0).astype(jnp.bfloat16)
            xs[s, i] = sum1(p, i, 1, half).astype(jnp.bfloat16)
        stage2[p] = [remote(ys.at[s], yr2.at[p], s2s.at[p, 0], s2r.at[p, 0], ydev),
                     remote(xs.at[s], xr2.at[p], s2s.at[p, 1], s2r.at[p, 1], xdev)]
        for copy in stage2[p]:
            copy.start()

    def do2(p):
        for copy in stage2[p]:
            copy.wait_recv()
        s = p % 2
        if p >= 2:
            for copy in stage3[p - 2]:
                copy.wait_send()
        x3s[s] = (sum1(p, 0, 1, 0) + yr2[p, 1].astype(F32)).astype(jnp.bfloat16)
        y3s[s] = (sum1(p, 1, 0, half) + xr2[p, 1].astype(F32)).astype(jnp.bfloat16)
        stage3[p] = [remote(x3s.at[s], x3r.at[p], s3s.at[p, 0], s3r.at[p, 0], xdev),
                     remote(y3s.at[s], y3r.at[p], s3s.at[p, 1], s3r.at[p, 1], ydev)]
        for copy in stage3[p]:
            copy.start()

    def do3(p):
        for copy in stage3[p]:
            copy.wait_recv()
        s = p % 2
        left = sum1(p, 0, 0, 0) + yr2[p, 0].astype(F32) + x3r[p].astype(F32)
        right = sum1(p, 0, 0, half) + xr2[p, 0].astype(F32) + y3r[p].astype(F32)
        if p >= 3:
            stage4[p - 2].wait_send()
        if p == 0:
            zr4[0, :, 0:half] = left.astype(jnp.bfloat16)
            zr4[0, :, half:cols] = right.astype(jnp.bfloat16)
        else:
            zsb[s, :, 0:half] = left.astype(jnp.bfloat16)
            zsb[s, :, half:cols] = right.astype(jnp.bfloat16)
            stage4[p] = remote(zsb.at[s], zr4.at[nz - p], s4s.at[p], s4r.at[nz - p], zdev(p))
            stage4[p].start()

    def up(p, k):
        s = p % 2
        dense = xbuf[s, :, :, width_all:].reshape(2 * rows, -1).astype(F32)
        lane = lax.broadcasted_iota(jnp.int32, dense.shape, 1)
        scale = jnp.sum(jnp.where(lane == e * exp_local + k, dense, 0.0), axis=1, keepdims=True)
        deep = 1024
        acc[...] = jnp.zeros_like(acc)

        @pl.loop(0, width_all // deep)
        def _(i):
            at = pl.ds(pl.multiple_of(i * deep, LANE), deep)
            xa = xbuf[s, :, :, at].reshape(2 * rows, deep)
            acc[0] += jnp.dot(xa, gw[k, at, :], preferred_element_type=F32)
            acc[1] += jnp.dot(xa, uw[k, at, :], preferred_element_type=F32)

        gate, upp = acc[0], acc[1]
        hid[:, k * ff:(k + 1) * ff] = (jax.nn.silu(gate) * upp * scale).astype(jnp.bfloat16)

    def down(p, piece, pieces):
        tile = 512
        count = width_all // tile // pieces

        @pl.loop(0, count)
        def _(i):
            at = pl.ds(pl.multiple_of((piece * count + i) * tile, LANE), tile)
            value = jnp.dot(hid[...], dw[:, at], preferred_element_type=F32)
            part[p % 2, :, :, at] = value.astype(jnp.bfloat16).reshape(2, rows, tile)

    send_own()
    own_load = pltpu.make_async_copy(x_ref, xbuf.at[0, 0], lsem.at[2])
    own_load.start()
    take_x(0)
    if nz > 1:
        take_z(1)
    take_y(0)
    take_c(0)
    own_load.wait()
    for copy in weights:
        copy.wait()
    for p in range(nz):
        load_wait(p)
        up(p, 0)
        if p + 2 < nz:
            take_z(p + 2)
        if p >= 1:
            do1(p - 1)
        for k in range(1, exp_local):
            up(p, k)
        if p + 1 < nz:
            take_x(p + 1)
        if p >= 1:
            do2(p - 1)
        down(p, 0, 2)
        if p + 1 < nz:
            take_y(p + 1)
        if p >= 1:
            do3(p - 1)
        down(p, 1, 2)
        send1(p)
        if p + 1 < nz:
            take_c(p + 1)
    do1(nz - 1)
    do2(nz - 1)
    do3(nz - 1)
    total = zr4[0].astype(F32)
    for p in range(1, nz):
        remote(zr4.at[p], zr4.at[p], s4s.at[0], s4r.at[p], xdev).wait_recv()
        total = total + zr4[p].astype(F32)
    out_ref[...] = total.astype(jnp.bfloat16)
    for copy in sends:
        copy.wait_send()
    for p in range(max(0, nz - 2), nz):
        for copy in stage2[p] + stage3[p]:
            copy.wait_send()
    for p in range(max(1, nz - 2), nz):
        stage4[p].wait_send()


def local(tokens, expert_ids, combine_weights, gate_weight, up_weight, down_weight):
    rows, width_all = tokens.shape
    exp_local, _, ff = gate_weight.shape
    n_expert = lax.axis_size("expert")
    n_width = lax.axis_size("width")
    assert n_width == 4 and n_expert % 2 == 0
    nz = n_expert // 2
    experts_all = exp_local * n_expert
    lanes = -(-experts_all // (2 * LANE)) * 2 * LANE
    cols = width_all // n_width
    tiles = (width_all + lanes) // LANE
    shared = tiles * 5 // 34
    if (tiles - 4 * shared) % 2:
        raise ValueError("tiles")
    single = (tiles - 4 * shared) // 2 * LANE
    shared = shared * LANE
    named = expert_ids[:, :, None] == jnp.arange(lanes, dtype=jnp.int32)
    dense = jnp.sum(jnp.where(named, combine_weights[:, :, None], 0.0), axis=1)
    wide = jnp.concatenate([tokens, dense.astype(jnp.bfloat16)], axis=1)
    total = width_all + lanes
    half = cols // 2
    bf = jnp.bfloat16
    dma = pltpu.SemaphoreType.DMA
    anyspace = pl.BlockSpec(memory_space=pl.ANY)
    out, _ = pl.pallas_call(
        functools.partial(kernel, nz, shared, single, exp_local, rows, width_all, ff),
        out_shape=(jax.ShapeDtypeStruct((rows, cols), bf),
                   jax.ShapeDtypeStruct((n_expert, rows, total), bf)),
        in_specs=[anyspace] * 4,
        out_specs=(pl.BlockSpec(memory_space=pltpu.VMEM), anyspace),
        scratch_shapes=[
            pltpu.VMEM(gate_weight.shape, bf),
            pltpu.VMEM(up_weight.shape, bf),
            pltpu.VMEM((exp_local * ff, width_all), bf),
            pltpu.VMEM((2, 2, rows, total), bf),
            pltpu.VMEM((2, 2 * rows, ff), F32),
            pltpu.VMEM((2 * rows, exp_local * ff), bf),
            pltpu.VMEM((2, 2, rows, width_all), bf),
            pltpu.VMEM((nz, 2, 2, rows, cols), bf),
            pltpu.VMEM((2, 2, rows, half), bf),
            pltpu.VMEM((2, 2, rows, half), bf),
            pltpu.VMEM((nz, 2, rows, half), bf),
            pltpu.VMEM((nz, 2, rows, half), bf),
            pltpu.VMEM((2, rows, half), bf),
            pltpu.VMEM((2, rows, half), bf),
            pltpu.VMEM((nz, rows, half), bf),
            pltpu.VMEM((nz, rows, half), bf),
            pltpu.VMEM((2, rows, cols), bf),
            pltpu.VMEM((nz, rows, cols), bf),
            dma((3,)), dma((3,)),
            dma((nz, 2)), dma((nz, 2)), dma((nz, 2)), dma((nz, 2)),
            dma((nz, 2)), dma((nz, 2)), dma((nz, 2, 3)), dma((nz, 2, 3)),
            dma((nz, 2)), dma((nz, 2)), dma((nz, 2)), dma((nz, 2)),
            dma((nz, 2)), dma((nz, 2)), dma((nz,)), dma((nz,)),
        ],
        compiler_params=pltpu.CompilerParams(
            collective_id=0, has_side_effects=True, vmem_limit_bytes=67_043_328),
    )(wide, gate_weight, up_weight, down_weight.reshape(exp_local * ff, width_all))
    return out


def solution(mesh):
    placed = (
        P("expert", None),
        P("expert", None),
        P("expert", None),
        P("expert", None, "width"),
        P("expert", None, "width"),
        P("expert", "width", None),
    )
    return jax.shard_map(
        local, mesh=mesh, in_specs=placed, out_specs=P("expert", "width"), check_vma=False
    )
```

time: 309 us -> 152 us (0.49)
  waiting for transfers between devices: 198 us -> 0 us
  Pallas kernels: 0 us -> 146 us
  matrix products: 38.1 us -> 0 us
  blocking collectives: 32.4 us -> 0 us
  local copies, waits for them, and re-layouts: 26.3 us -> 3.24 us
  between operations: 13.4 us -> 0.01 us
    reduce_scatter x1 -> x0, waiting for transfers between devices: 149 us -> none  [local(): lax.psum_scatter(blocks, ('expert', 'width'), scatter_dimension=0, tiled=...]
    pallas_call x0 -> x1, Pallas kernels: none -> 146 us  [local(): pl.pallas_call(functools.partial(kernel, nz, shared, single, exp_local, r...]
    all_gather x1 -> x0, waiting for transfers between devices: 48.4 us -> none  [local(): every = lax.all_gather(own, ('expert', 'width'), axis=0, tiled=True)]
    dot_general x2 -> x0, matrix products: 38.1 us -> none  [the longest x1 26 us: local(): jnp.einsum('ktf,kfd->td', hidden, down_weight, preferred_element_type=jnp...]
    all_gather x1 -> x0, blocking collectives: 32.4 us -> none  [local(): dense = lax.all_gather(dense, 'expert', axis=0, tiled=True)]
    reshape x1 -> x0, local copies, waits for them, and re-layouts: 14.6 us -> none  [local(): partial_value.reshape(n_expert, rows, n_width, cols).transpose(0, 2, 1, 3)]
    transpose x2 -> x0, local copies, waits for them, and re-layouts: 9.78 us -> none  [the longest x1 9.77 us: local(): partial_value.reshape(n_expert, rows, n_width, cols).transpose(0, 2, 1, 3)]
  transfers between devices with their start and end apart: 2 -> 0, of which waited for: 2 -> 0; matrix products, arithmetic and copies ran while one was open for 0% -> 0% of each run, Pallas kernels for 0% -> 0%
where the time goes in v2:
time: 152 us
  Pallas kernels  146 us (96%)
  local copies, waits for them, and re-layouts  3.24 us (2%)
  other arithmetic  2.79 us (2%)
    pallas_call x1, Pallas kernels, local(): pl.pallas_call(functools.partial(kernel, nz, shared, single, exp_local, r...  146 us
    unnamed x3, local copies, waits for them, and re-layouts  3.24 us

profile of v2, /device:TPU:0, one launch (start us, length us, event | category | flops | bytes accessed | tf_op | source)
XLA Modules:
  0.0 151.9 jit_solution(1065421353427427424)
XLA Ops:
  0.0 0.8 copy.9
  0.8 0.8 copy.10
  1.6 0.4 select_reduce_fusion
  2.0 2.4 %pad_maximum_fusion.x_ref = bf16[128,4352]{1,0:T(8,128)(2,1)} fusion(bf16[128,256]{1,0:T(8,128)(2,1)S(1)} %select_reduce_fusion, bf16[128,4096]{1,0:T(8,128)(2,1)} %param.6), kind=kLoop, calls=%fused_computation | loop fusion | flops 2228224 | bytes 2228224 | tf_op jit(solution)/shard_map/concatenate | solution.py:282
  4.4 145.9 %shard_map.64 = (bf16[128,1024]{1,0:T(8,128)(2,1)}, bf16[8,128,4352]{2,1,0:T(8,128)(2,1)}) custom-call(bf16[128,4352]{1,0:T(8,128)(2,1)} %pad_maximum_fusion.x_ref, bf16[2,4096,384]{2,1,0:T(8,128)(2,1)} %g_hbm.1, bf16[2,4096,384]{2,1,0:T(8,128)(2,1)} %u_hbm.1, bf16[768,4096]{1,0:T(8,128)(2,1)} %bitcast.1), custom_call_target="tpu_custom_call" | custom-call | tf_op jit(solution)/shard_map/pallas_call | solution.py:288
  150.3 1.7 %copy.12 = bf16[128,1024]{1,0:T(8,128)(2,1)} copy(bf16[128,1024]{1,0:T(8,128)(2,1)} %get-tuple-element.6) | data formatting | bytes 524288

commit v3 on v2

--- a/solution.py
+++ b/solution.py
@@ -227,24 +227,26 @@
         up(p, 0)
         if p + 2 < nz:
             take_z(p + 2)
-        if p >= 1:
-            do1(p - 1)
+        if p >= 2:
+            do3(p - 2)
         for k in range(1, exp_local):
             up(p, k)
         if p + 1 < nz:
             take_x(p + 1)
         if p >= 1:
-            do2(p - 1)
+            do1(p - 1)
         down(p, 0, 2)
         if p + 1 < nz:
             take_y(p + 1)
-        if p >= 1:
-            do3(p - 1)
         down(p, 1, 2)
         send1(p)
         if p + 1 < nz:
             take_c(p + 1)
+        if p >= 1:
+            do2(p - 1)
     do1(nz - 1)
+    if nz >= 2:
+        do3(nz - 2)
     do2(nz - 1)
     do3(nz - 1)
     total = zr4[0].astype(F32)

time: 152 us -> 138 us (0.908)
  Pallas kernels: 146 us -> 131 us
    pallas_call x1, Pallas kernels: 146 us -> 131 us  [local(): pl.pallas_call(functools.partial(kernel, nz, shared, single, exp_local, r...]
where the time goes in v3:
time: 138 us; the launch traced here: 137 us
  Pallas kernels  131 us (95%)
  local copies, waits for them, and re-layouts  3.24 us (2%)
  other arithmetic  2.79 us (2%)
    pallas_call x1, Pallas kernels, local(): pl.pallas_call(functools.partial(kernel, nz, shared, single, exp_local, r...  131 us
    unnamed x3, local copies, waits for them, and re-layouts  3.24 us

profile of v3, /device:TPU:0, one launch (start us, length us, event | category | flops | bytes accessed | tf_op | source)
XLA Modules:
  0.0 137.5 jit_solution(8229271847331570913)
XLA Ops:
  0.0 0.8 copy.9
  0.8 0.8 copy.10
  1.6 0.4 select_reduce_fusion
  2.0 2.4 %pad_maximum_fusion.x_ref = bf16[128,4352]{1,0:T(8,128)(2,1)} fusion(bf16[128,256]{1,0:T(8,128)(2,1)S(1)} %select_reduce_fusion, bf16[128,4096]{1,0:T(8,128)(2,1)} %param.6), kind=kLoop, calls=%fused_computation | loop fusion | flops 2228224 | bytes 2228224 | tf_op jit(solution)/shard_map/concatenate | solution.py:284
  4.4 131.4 %shard_map.64 = (bf16[128,1024]{1,0:T(8,128)(2,1)}, bf16[8,128,4352]{2,1,0:T(8,128)(2,1)}) custom-call(bf16[128,4352]{1,0:T(8,128)(2,1)} %pad_maximum_fusion.x_ref, bf16[2,4096,384]{2,1,0:T(8,128)(2,1)} %g_hbm.1, bf16[2,4096,384]{2,1,0:T(8,128)(2,1)} %u_hbm.1, bf16[768,4096]{1,0:T(8,128)(2,1)} %bitcast.1), custom_call_target="tpu_custom_call" | custom-call | tf_op jit(solution)/shard_map/pallas_call | solution.py:290
  135.8 1.7 %copy.12 = bf16[128,1024]{1,0:T(8,128)(2,1)} copy(bf16[128,1024]{1,0:T(8,128)(2,1)} %get-tuple-element.6) | data formatting | bytes 524288
